TPU v7x, 512 devices: a whole 4x8x8 slice. The times are simulated.
512 devices in a mesh: seq: 32 (over x, y), grp: 16 (over z, core).
Axes of the slice: x: 4, y: 8, z: 8, core: 2. Of those that a mesh axis runs over, the one named last changes fastest.
Arguments:
- normed_hidden_input: bfloat16 [65536, 4096], P(('grp', 'seq')), may hold values from -6 to 6
- frozen_query_rows: bfloat16 [65536, 4096], P(('grp', 'seq')), may hold values from -16 to 16
- frozen_key_rows: bfloat16 [65536, 1024], P(('grp', 'seq')), may hold values from -16 to 16
- attention_output_gradient: bfloat16 [65536, 4096], P(('grp', 'seq')), may hold values from -0.15625 to 0.15625
- adapter_down_weight: bfloat16 [256, 64, 4096], P('grp', None, 'seq'), may hold values from -0.09375 to 0.09375
- adapter_up_weight: bfloat16 [256, 64, 1024], P('grp', 'seq'), may hold values from -0.75 to 0.75
- segment_adapter_index: int32 [16, 16], replicated, may hold values from 0 to 255, as said below
- segment_block_count: int32 [16, 16], replicated, may hold values from 1 to 16, 32 in all within a row
- adapter_row_index: int32 [256], replicated, may hold values from 0 to 255, as said below
Outputs:
- down_grad: float32 [256, 64, 4096], P('grp', None, 'seq')
- up_grad: float32 [256, 64, 1024], P('grp', 'seq')
Inputs may be any that keep to these rules, and one draw needn't show every extreme that they name: A permutation: adapter a is held in row adapter_row_index[a] of adapter_down_weight and adapter_up_weight. `segment_adapter_index`: call rows g * 16 to (g + 1) * 16 - 1 of adapter_down_weight the rows of index g of grp. In each sequence at most 2 segments use adapters held in the rows of one index of grp, and in every sequence some index holds exactly 2 of them. Tenants may repeat within and across sequences. `segment_block_count`: each row sums to 32; in each row some segment has exactly 16 blocks.
All inputs are finite; a program needn't handle non-finite values.
Results may differ from a plain program's by a relative error of at most 0.0056.
Values may be sent and summed in bfloat16 or wider, within the bound.
No kernel may reach another device: no remote copies, remote signals or barrier semaphores. Data moves between devices by JAX's collectives and lax.ppermute only.
A program may use at most 64 MiB of HBM per device.

v0:
```python
import math
import jax
import jax.numpy as jnp
from jax import lax
from jax.sharding import PartitionSpec as P

HEAD_DIM = 128
BLOCK = 128
QROWS = 512
adapter_scale = 2.0


def attend_head(query_head, key_head, grad_head, segment_ids, query_rows, reach):
    length, head_width = query_head.shape
    padded_keys = jnp.concatenate([jnp.zeros((reach, head_width), key_head.dtype), key_head], 0)
    padded_ids = jnp.concatenate([jnp.full((reach,), -1, jnp.int32), segment_ids], 0)
    window = query_rows + reach
    factor = 1.0 / math.sqrt(head_width)

    def one_block(totals, number):
        offset = number * query_rows
        query_block = lax.dynamic_slice_in_dim(query_head, offset, query_rows, 0)
        grad_block = lax.dynamic_slice_in_dim(grad_head, offset, query_rows, 0)
        key_block = lax.dynamic_slice_in_dim(padded_keys, offset, window, 0)
        key_ids = lax.dynamic_slice_in_dim(padded_ids, offset, window, 0)
        query_ids = lax.dynamic_slice_in_dim(segment_ids, offset, query_rows, 0)
        scores = jnp.dot(query_block, key_block.T, preferred_element_type=jnp.float32) * factor
        query_pos = offset + jnp.arange(query_rows, dtype=jnp.int32)
        key_pos = offset - reach + jnp.arange(window, dtype=jnp.int32)
        allowed = (key_ids[None, :] == query_ids[:, None]) & (
            key_pos[None, :] <= query_pos[:, None]
        )
        scores = jnp.where(allowed, scores, jnp.float32(-1e30))
        highest = jnp.max(scores, axis=1, keepdims=True)
        expo = jnp.exp(scores - highest)
        probabilities = (expo / jnp.sum(expo, axis=1, keepdims=True)).astype(jnp.bfloat16)
        contribution = jnp.dot(probabilities.T, grad_block, preferred_element_type=jnp.float32)
        current = lax.dynamic_slice_in_dim(totals, offset, window, 0)
        totals = lax.dynamic_update_slice_in_dim(totals, current + contribution, offset, 0)
        return (totals, None)

    initial = jnp.zeros((length + reach, head_width), jnp.float32)
    totals, _ = lax.scan(one_block, initial, jnp.arange(length // query_rows, dtype=jnp.int32))
    return totals[reach:].astype(jnp.bfloat16)


def local(
    normed_hidden_input,
    frozen_query_rows,
    frozen_key_rows,
    attention_output_gradient,
    adapter_down_weight,
    adapter_up_weight,
    segment_adapter_index,
    segment_block_count,
    adapter_row_index,
):
    group_count = lax.axis_size("grp")
    shard_count = lax.axis_size("seq")
    group_index = lax.axis_index("grp")
    tokens_here, model_width = normed_hidden_input.shape
    portion_width = adapter_down_weight.shape[2]
    resident_adapters, rank_overall = (adapter_down_weight.shape[0], adapter_down_weight.shape[1])
    rank_portion, value_projection_width = (adapter_up_weight.shape[1], adapter_up_weight.shape[2])
    segments = segment_adapter_index.shape[1]
    capacity = max(2, (segments + group_count - 1) // group_count)
    seq_length = tokens_here * shard_count
    block_total = seq_length // BLOCK
    block_here = tokens_here // BLOCK
    reach = min(16, seq_length // (2 * BLOCK)) * BLOCK
    head_total = frozen_query_rows.shape[1] // HEAD_DIM
    kv_heads = value_projection_width // HEAD_DIM
    heads_here = head_total // shard_count
    group_size = head_total // kv_heads
    slot_total = group_count * capacity
    adapter_ids = jnp.arange(adapter_row_index.shape[0], dtype=jnp.int32)
    slot_of = jnp.sum(
        jnp.where(segment_adapter_index[:, :, None] == adapter_ids, adapter_row_index, 0), axis=2
    )
    owner_group = slot_of // resident_adapters
    local_slot = slot_of % resident_adapters
    order_ids = jnp.arange(segments, dtype=jnp.int32)
    earlier = order_ids[:, None] > order_ids[None, :]
    same_owner = owner_group[:, :, None] == owner_group[:, None, :]
    rank_in_owner = jnp.sum((same_owner & earlier[None]).astype(jnp.int32), axis=2)
    placement = owner_group * capacity + rank_in_owner
    capacity_ids = jnp.arange(capacity, dtype=jnp.int32)
    local_ids = jnp.arange(resident_adapters, dtype=jnp.int32)
    picks = (
        (owner_group == group_index)[:, :, None, None]
        & (rank_in_owner[:, :, None, None] == capacity_ids[:, None])
        & (local_slot[:, :, None, None] == local_ids)
    )
    chooser = jnp.sum(picks.astype(jnp.float32), axis=1)
    selector_half = chooser.astype(jnp.bfloat16)
    send_down = jnp.einsum(
        "pgl,lut->pgut", selector_half, adapter_down_weight, preferred_element_type=jnp.float32
    ).astype(jnp.bfloat16)
    send_up = jnp.einsum(
        "gyv,vmf->gymf", selector_half, adapter_up_weight, preferred_element_type=jnp.float32
    ).astype(jnp.bfloat16)
    fetched_down, fetched_up = (
        lax.all_to_all(send_down, "grp", split_axis=0, concat_axis=0, tiled=True),
        lax.all_to_all(send_up, "grp", split_axis=0, concat_axis=0, tiled=True),
    )
    own_blocks = segment_block_count[group_index]
    ends = jnp.cumsum(own_blocks)
    block_seg = jnp.sum(
        (jnp.arange(block_total, dtype=jnp.int32)[:, None] >= ends[None, :]).astype(jnp.int32),
        axis=1,
    )
    own_place = placement[group_index]
    block_place = jnp.sum(
        jnp.where(block_seg[:, None] == order_ids[None, :], own_place[None, :], 0), axis=1
    )
    block_pick = block_place[:, None] == jnp.arange(slot_total, dtype=jnp.int32)[None, :]
    pick_half = block_pick.astype(jnp.bfloat16)
    segment_ids = jnp.broadcast_to(block_seg[:, None], (block_total, BLOCK)).reshape(seq_length)
    block_down_weight = jnp.einsum(
        "bn,nrd->brd",
        pick_half,
        fetched_down.reshape(slot_total, rank_overall, portion_width),
        preferred_element_type=jnp.float32,
    ).astype(jnp.bfloat16)
    block_up_rows = jnp.einsum(
        "bn,nre->bre",
        pick_half,
        fetched_up.reshape(slot_total, rank_portion, value_projection_width),
        preferred_element_type=jnp.float32,
    ).astype(jnp.bfloat16)
    features = lax.all_to_all(normed_hidden_input, "seq", split_axis=1, concat_axis=0, tiled=True)
    amount = lax.axis_size("seq") * tokens_here
    token_rows = features.reshape(amount // BLOCK, BLOCK, portion_width)
    reduced_rank_part = (
        lax.psum_scatter(
            jnp.einsum(
                "jyw,jaw->jya", token_rows, block_down_weight, preferred_element_type=jnp.float32
            ).reshape(amount, rank_overall),
            "seq",
            scatter_dimension=0,
            tiled=True,
        )
        .astype(jnp.bfloat16)
        .reshape(block_here, BLOCK, rank_overall)
    )
    near_up = lax.all_to_all(block_up_rows, "seq", split_axis=0, concat_axis=1, tiled=True)
    query_grid = frozen_query_rows.reshape(tokens_here, shard_count, heads_here, HEAD_DIM)
    key_grid = jnp.repeat(
        frozen_key_rows.reshape(tokens_here, kv_heads, HEAD_DIM), group_size, axis=1
    ).reshape(tokens_here, shard_count, heads_here, HEAD_DIM)
    grad_grid = attention_output_gradient.reshape(tokens_here, shard_count, heads_here, HEAD_DIM)
    query_all = lax.all_to_all(query_grid, "seq", split_axis=1, concat_axis=0, tiled=True)
    key_all = lax.all_to_all(key_grid, "seq", split_axis=1, concat_axis=0, tiled=True)
    grad_all = lax.all_to_all(grad_grid, "seq", split_axis=1, concat_axis=0, tiled=True)

    def per_head(triple):
        return attend_head(triple[0], triple[1], triple[2], segment_ids, QROWS, reach)

    stacked = (
        jnp.moveaxis(query_all[:, 0], 1, 0),
        jnp.moveaxis(key_all[:, 0], 1, 0),
        jnp.moveaxis(grad_all[:, 0], 1, 0),
    )
    result = lax.map(per_head, stacked)
    head_grads = jnp.moveaxis(result, 0, 1)[:, None]
    token_grads = lax.all_to_all(head_grads, "seq", split_axis=0, concat_axis=1, tiled=True)
    value_grad = jnp.sum(
        token_grads.reshape(tokens_here, kv_heads, group_size, HEAD_DIM), axis=2, dtype=jnp.float32
    )
    value_row_blocks = value_grad.reshape(block_here, BLOCK, value_projection_width).astype(
        jnp.bfloat16
    )
    up_weight_terms = adapter_scale * jnp.einsum(
        "fvg,fvn->fgn", reduced_rank_part, value_row_blocks, preferred_element_type=jnp.float32
    )
    backward_rank_part = (
        adapter_scale
        * jnp.einsum("vaw,vpw->vap", value_row_blocks, near_up, preferred_element_type=jnp.float32)
    ).astype(jnp.bfloat16)
    all_low = lax.all_gather(
        backward_rank_part.reshape(tokens_here, rank_overall), "seq", axis=0, tiled=True
    )
    back_down = jnp.einsum(
        "jcy,jct->jyt",
        all_low.reshape(block_total, BLOCK, rank_overall),
        features.reshape(block_total, BLOCK, portion_width),
        preferred_element_type=jnp.float32,
    )
    back_up = lax.all_to_all(up_weight_terms, "seq", split_axis=1, concat_axis=0, tiled=True)
    pick_full = block_pick.astype(jnp.float32)
    slot_down = jnp.einsum("bn,brd->nrd", pick_full, back_down, precision=lax.Precision.HIGHEST)
    slot_up = jnp.einsum("bn,bre->nre", pick_full, back_up, precision=lax.Precision.HIGHEST)
    return_down, return_up = (
        lax.all_to_all(
            slot_down.reshape(group_count, capacity, rank_overall, portion_width),
            "grp",
            split_axis=0,
            concat_axis=0,
            tiled=True,
        ),
        lax.all_to_all(
            slot_up.reshape(group_count, capacity, rank_portion, value_projection_width),
            "grp",
            split_axis=0,
            concat_axis=0,
            tiled=True,
        ),
    )
    down_grad = jnp.einsum("nca,ncrd->ard", chooser, return_down, precision=lax.Precision.HIGHEST)
    up_grad = jnp.einsum("nca,ncre->are", chooser, return_up, precision=lax.Precision.HIGHEST)
    return (down_grad, up_grad)


def solution(mesh):
    return jax.shard_map(
        local,
        mesh=mesh,
        in_specs=(
            P(("grp", "seq"), None),
            P(("grp", "seq"), None),
            P(("grp", "seq"), None),
            P(("grp", "seq"), None),
            P("grp", None, "seq"),
            P("grp", "seq", None),
            P(),
            P(),
            P(),
        ),
        out_specs=(P("grp", None, "seq"), P("grp", "seq", None)),
        check_vma=False,
    )
```

profile of v0, /device:TPU:1, one launch (start us, length us, event | category | flops | bytes accessed | tf_op | source)
XLA Modules:
  0.0 591.7 jit_solution(1120349917430718640)
XLA Ops:
  11.0 11.8 %all-to-all-start.4 = ((bf16[16,2,2,1024]{3,2,1,0:T(2,128)(2,1)}), bf16[16,2,2,1024]{3,2,1,0:T(2,128)(2,1)S(1)}, u32[]{:S(2)}, u32[]{:S(2)}) async-start(bf16[16,2,2,1024]{3,2,1,0:T(2,128)(2,1)} %copy.109), calls=%async_computation.4 | async-start | bytes 262144 | tf_op jit(solution)/shard_map/all_to_all | solution.py:104
  25.0 7.0 %all-to-all-done.4 = bf16[16,2,2,1024]{3,2,1,0:T(2,128)(2,1)S(1)} async-done(((bf16[16,2,2,1024]{3,2,1,0:T(2,128)(2,1)}), bf16[16,2,2,1024]{3,2,1,0:T(2,128)(2,1)S(1)}, u32[]{:S(2)}, u32[]{:S(2)}) %all-to-all-start.4) | async-done | bytes 131104 | tf_op jit(solution)/shard_map/all_to_all | solution.py:104
  32.0 3.5 all-to-all-start.8
  35.5 16.8 %all-to-all-done.8 = bf16[16,2,64,128]{3,2,1,0:T(8,128)(2,1)S(1)} async-done(((bf16[16,2,64,128]{3,2,1,0:T(8,128)(2,1)}), bf16[16,2,64,128]{3,2,1,0:T(8,128)(2,1)S(1)}, u32[]{:S(2)}, u32[]{:S(2)}) %all-to-all-start.8) | async-done | bytes 524320 | tf_op jit(solution)/shard_map/all_to_all | solution.py:103
  53.5 9.7 %all-to-all-start.1 = ((bf16[128,32,1,128]{3,0,2,1:T(8,128)(2,1)}), bf16[128,32,1,128]{3,0,2,1:T(8,128)(2,1)S(1)}, u32[]{:S(2)}, u32[]{:S(2)}) async-start(bf16[128,32,1,128]{3,0,2,1:T(8,128)(2,1)} %bitcast.10), calls=%async_computation.1 | async-start | bytes 2097152 | tf_op jit(solution)/shard_map/all_to_all | solution.py:153
  63.2 1.6 copy.103
  66.2 25.2 %all-to-all-done.1 = bf16[128,32,1,128]{3,0,2,1:T(8,128)(2,1)S(1)} async-done(((bf16[128,32,1,128]{3,0,2,1:T(8,128)(2,1)}), bf16[128,32,1,128]{3,0,2,1:T(8,128)(2,1)S(1)}, u32[]{:S(2)}, u32[]{:S(2)}) %all-to-all-start.1) | async-done | bytes 1048608 | tf_op jit(solution)/shard_map/all_to_all | solution.py:153
  91.4 5.6 all-to-all-start.2
  97.0 1.6 copy.100
  99.9 22.2 %all-to-all-done.2 = bf16[128,32,1,128]{3,0,2,1:T(8,128)(2,1)} async-done(((bf16[128,32,1,128]{3,0,2,1:T(8,128)(2,1)}), bf16[128,32,1,128]{3,0,2,1:T(8,128)(2,1)}, u32[]{:S(2)}, u32[]{:S(2)}) %all-to-all-start.2) | async-done | bytes 1048608 | tf_op jit(solution)/shard_map/all_to_all | solution.py:154
  122.2 8.1 %all-to-all-start = ((bf16[128,32,1,128]{3,0,2,1:T(8,128)(2,1)}), bf16[128,32,1,128]{3,0,2,1:T(8,128)(2,1)}, u32[]{:S(2)}, u32[]{:S(2)}) async-start(bf16[128,32,1,128]{3,0,2,1:T(8,128)(2,1)} %copy.101), calls=%async_computation | async-start | bytes 2097152 | tf_op jit(solution)/shard_map/all_to_all | solution.py:152
  131.2 1.6 copy.112
  135.8 19.1 %all-to-all-done = bf16[128,32,1,128]{3,0,2,1:T(8,128)(2,1)} async-done(((bf16[128,32,1,128]{3,0,2,1:T(8,128)(2,1)}), bf16[128,32,1,128]{3,0,2,1:T(8,128)(2,1)}, u32[]{:S(2)}, u32[]{:S(2)}) %all-to-all-start) | async-done | bytes 1048608 | tf_op jit(solution)/shard_map/all_to_all | solution.py:152
  154.9 8.6 %all-to-all-start.6 = ((bf16[128,32,128]{2,0,1:T(8,128)(2,1)}), bf16[128,32,128]{2,0,1:T(8,128)(2,1)S(1)}, u32[]{:S(2)}, u32[]{:S(2)}) async-start(bf16[128,32,128]{2,0,1:T(8,128)(2,1)} %copy.113), calls=%async_computation.6 | async-start | bytes 2097152 | tf_op jit(solution)/shard_map/all_to_all | solution.py:131
  163.5 1.9 broadcast.202
  165.3 67.9 %while.19 = (s32[]{:T(128)}, f32[6144,128]{1,0:T(8,128)}, s32[8]{0:T(128)S(1)}, s32[6144]{0:T(1024)S(1)}, s32[4096]{0:T(1024)S(1)}, /*index=5*/bf16[4096,128]{1,...) while((s32[]{:T(128)}, f32[6144,128]{1,0:T(8,128)}, ...), condition=%wide.region_9.10_spmd, body=%wide.region_6.9_spmd.sunk | while | flops 685836288 | bytes 19343620 | solution.py:43
  166.8 2.4 fusion.62
  170.0 3.8 fusion.64
  175.2 2.4 fusion.62
  178.5 3.8 fusion.64
  183.7 2.4 fusion.62
  187.0 3.8 fusion.64
  192.2 2.4 fusion.62
  195.5 3.8 fusion.64
  200.7 2.4 fusion.62
  204.0 3.8 fusion.64
  209.2 2.4 fusion.62
  212.5 3.8 fusion.64
  217.7 2.4 fusion.62
  221.0 3.8 fusion.64
  226.2 2.4 fusion.62
  229.5 3.8 fusion.64
  233.3 1.7 fusion.9
  235.5 1.4 reduce.3
  238.1 9.2 %all-to-all-start.3 = ((bf16[32,2,8192]{2,1,0:T(2,128)(2,1)}), bf16[32,2,8192]{2,1,0:T(2,128)(2,1)S(1)}, u32[]{:S(2)}, u32[]{:S(2)}) async-start(bf16[32,2,8192]{2,1,0:T(2,128)(2,1)} %reshape.260), calls=%async_computation.3 | async-start | bytes 2097152 | tf_op jit(solution)/shard_map/all_to_all | solution.py:166
  247.6 1.9 convolution_bitcast_fusion
  251.6 20.3 %all-to-all-done.3 = bf16[32,2,8192]{2,1,0:T(2,128)(2,1)S(1)} async-done(((bf16[32,2,8192]{2,1,0:T(2,128)(2,1)}), bf16[32,2,8192]{2,1,0:T(2,128)(2,1)S(1)}, u32[]{:S(2)}, u32[]{:S(2)}) %all-to-all-start.3) | async-done | bytes 1048608 | tf_op jit(solution)/shard_map/all_to_all | solution.py:166
  272.9 8.3 %all-to-all-start.5 = ((bf16[32,2,1024]{2,1,0:T(2,128)(2,1)}), bf16[32,2,1024]{2,1,0:T(2,128)(2,1)S(1)}, u32[]{:S(2)}, u32[]{:S(2)}) async-start(bf16[32,2,1024]{2,1,0:T(2,128)(2,1)} %copy.111), calls=%async_computation.5 | async-start | bytes 262144 | tf_op jit(solution)/shard_map/all_to_all | solution.py:146
  281.3 4.3 reshape.261
  286.7 1.4 reduce_sum.74
  288.3 176.5 %reduce-scatter.2.cloned.1.call-done = f32[128,64]{0,1:T(8,128)} async-done(((f32[4096,64]{0,1:T(8,128)}), f32[128,64]{0,1:T(8,128)}) %reduce-scatter.2.cloned.1.call-update) | async-done | bytes 32784 | tf_op jit(solution)/shard_map/reduce_scatter | solution.py:135
  466.8 6.5 %all-to-all-start.9 = ((f32[1,64,1024]{2,0,1:T(1,128)}), f32[1,64,1024]{2,0,1:T(1,128)S(1)}, u32[]{:S(2)}, u32[]{:S(2)}) async-start(f32[1,64,1024]{2,0,1:T(1,128)} %copy.126), calls=%async_computation.10 | async-start | bytes 524288 | tf_op jit(solution)/shard_map/all_to_all | solution.py:189
  473.5 39.6 %all_gather.3 = bf16[4096,64]{0,1:T(8,128)(2,1)S(1)} all-gather(bf16[128,64]{0,1:T(8,128)(2,1)S(1)} %fusion.8), channel_id=1, replica_groups=mesh['seq'=32,'grp'=16] {'seq'}, dimensions={0}, use_global_device_ids=true | all-gather | bytes 540672 | tf_op jit(solution)/shard_map/all_gather | solution.py:180
  515.2 25.0 %all-to-all-start.10 = ((f32[16,2,2,1024]{3,1,2,0:T(2,128)}), f32[16,2,2,1024]{3,1,2,0:T(2,128)S(1)}, u32[]{:S(2)}, u32[]{:S(2)}) async-start(f32[16,2,2,1024]{3,1,2,0:T(2,128)} %copy.128), calls=%async_computation.11 | async-start | bytes 524288 | tf_op jit(solution)/shard_map/all_to_all | solution.py:201
  541.9 1.5 copy.117
  543.5 8.4 %all-to-all-done.10 = f32[16,2,2,1024]{3,1,2,0:T(2,128)S(1)} async-done(((f32[16,2,2,1024]{3,1,2,0:T(2,128)}), f32[16,2,2,1024]{3,1,2,0:T(2,128)S(1)}, u32[]{:S(2)}, u32[]{:S(2)}) %all-to-all-start.10) | async-done | bytes 262176 | tf_op jit(solution)/shard_map/all_to_all | solution.py:201
  551.9 3.6 all-to-all-start.7
  556.7 26.0 %all-to-all-done.7 = f32[16,2,64,128]{3,1,2,0:T(2,128)S(1)} async-done(((f32[16,2,64,128]{3,1,2,0:T(2,128)}), f32[16,2,64,128]{3,1,2,0:T(2,128)S(1)}, u32[]{:S(2)}, u32[]{:S(2)}) %all-to-all-start.7) | async-done | bytes 1048608 | tf_op jit(solution)/shard_map/all_to_all | solution.py:194
  (115 shorter events, 42.4 us)
Async XLA Ops:
  7.2 28.3 %copy-start = (bf16[128,1024]{1,0:T(8,128)(2,1)S(1)}, bf16[128,1024]{1,0:T(8,128)(2,1)}, u32[]{:S(2)}) copy-start(bf16[128,1024]{1,0:T(8,128)(2,1)} %param.13) | copy-start | bytes 786436
  11.0 21.0 %all-to-all-start.4 = ((bf16[16,2,2,1024]{3,2,1,0:T(2,128)(2,1)}), bf16[16,2,2,1024]{3,2,1,0:T(2,128)(2,1)S(1)}, u32[]{:S(2)}, u32[]{:S(2)}) async-start(bf16[16,2,2,1024]{3,2,1,0:T(2,128)(2,1)} %copy.109), calls=%async_computation.4 | async-start | bytes 262144 | tf_op jit(solution)/shard_map/all_to_all | solution.py:104
  32.0 20.3 %all-to-all-start.8 = ((bf16[16,2,64,128]{3,2,1,0:T(8,128)(2,1)}), bf16[16,2,64,128]{3,2,1,0:T(8,128)(2,1)S(1)}, u32[]{:S(2)}, u32[]{:S(2)}) async-start(bf16[16,2,64,128]{3,2,1,0:T(8,128)(2,1)} %copy.122), calls=%async_computation.8 | async-start | bytes 1048576 | tf_op jit(solution)/shard_map/all_to_all | solution.py:103
  53.5 37.9 %all-to-all-start.1 = ((bf16[128,32,1,128]{3,0,2,1:T(8,128)(2,1)}), bf16[128,32,1,128]{3,0,2,1:T(8,128)(2,1)S(1)}, u32[]{:S(2)}, u32[]{:S(2)}) async-start(bf16[128,32,1,128]{3,0,2,1:T(8,128)(2,1)} %bitcast.10), calls=%async_computation.1 | async-start | bytes 2097152 | tf_op jit(solution)/shard_map/all_to_all | solution.py:153
  91.4 30.8 %all-to-all-start.2 = ((bf16[128,32,1,128]{3,0,2,1:T(8,128)(2,1)}), bf16[128,32,1,128]{3,0,2,1:T(8,128)(2,1)}, u32[]{:S(2)}, u32[]{:S(2)}) async-start(bf16[128,32,1,128]{3,0,2,1:T(8,128)(2,1)} %copy.104), calls=%async_computation.2 | async-start | bytes 2097152 | tf_op jit(solution)/shard_map/all_to_all | solution.py:154
  122.2 32.7 %all-to-all-start = ((bf16[128,32,1,128]{3,0,2,1:T(8,128)(2,1)}), bf16[128,32,1,128]{3,0,2,1:T(8,128)(2,1)}, u32[]{:S(2)}, u32[]{:S(2)}) async-start(bf16[128,32,1,128]{3,0,2,1:T(8,128)(2,1)} %copy.101), calls=%async_computation | async-start | bytes 2097152 | tf_op jit(solution)/shard_map/all_to_all | solution.py:152
  134.4 30.9 %copy-start.2 = (s32[32]{0:T(128)}, s32[32]{0:T(128)S(1)}, u32[]{:S(2)}) copy-start(s32[32]{0:T(128)S(1)} %select_reduce_fusion.1) | copy-start | bytes 388
  154.9 83.2 %all-to-all-start.6 = ((bf16[128,32,128]{2,0,1:T(8,128)(2,1)}), bf16[128,32,128]{2,0,1:T(8,128)(2,1)S(1)}, u32[]{:S(2)}, u32[]{:S(2)}) async-start(bf16[128,32,128]{2,0,1:T(8,128)(2,1)} %copy.113), calls=%async_computation.6 | async-start | bytes 2097152 | tf_op jit(solution)/shard_map/all_to_all | solution.py:131
  238.1 12.4 %copy-start.3 = (s32[32]{0:T(128)S(1)}, s32[32]{0:T(128)}, u32[]{:S(2)}) copy-start(s32[32]{0:T(128)} %copy-done.2) | copy-start | bytes 388
  238.1 33.8 %all-to-all-start.3 = ((bf16[32,2,8192]{2,1,0:T(2,128)(2,1)}), bf16[32,2,8192]{2,1,0:T(2,128)(2,1)S(1)}, u32[]{:S(2)}, u32[]{:S(2)}) async-start(bf16[32,2,8192]{2,1,0:T(2,128)(2,1)} %reshape.260), calls=%async_computation.3 | async-start | bytes 2097152 | tf_op jit(solution)/shard_map/all_to_all | solution.py:166
  247.4 217.5 %reduce-scatter.2.cloned.1.call-start = ((), (), s32[]{:S(2)}) async-start(), calls=%async_computation.12 | async-start | bytes 1081344 | tf_op jit(solution)/shard_map/reduce_scatter | solution.py:135
  271.9 1.0 copy-start.1
  272.9 193.9 %all-to-all-start.5 = ((bf16[32,2,1024]{2,1,0:T(2,128)(2,1)}), bf16[32,2,1024]{2,1,0:T(2,128)(2,1)S(1)}, u32[]{:S(2)}, u32[]{:S(2)}) async-start(bf16[32,2,1024]{2,1,0:T(2,128)(2,1)} %copy.111), calls=%async_computation.5 | async-start | bytes 262144 | tf_op jit(solution)/shard_map/all_to_all | solution.py:146
  286.7 227.2 %copy-start.4 = (s32[32]{0:T(128)S(1)}, s32[32]{0:T(128)}, u32[]{:S(2)}) copy-start(s32[32]{0:T(128)} %copy-done.2) | copy-start | bytes 388
  466.8 46.3 %all-to-all-start.9 = ((f32[1,64,1024]{2,0,1:T(1,128)}), f32[1,64,1024]{2,0,1:T(1,128)S(1)}, u32[]{:S(2)}, u32[]{:S(2)}) async-start(f32[1,64,1024]{2,0,1:T(1,128)} %copy.126), calls=%async_computation.10 | async-start | bytes 524288 | tf_op jit(solution)/shard_map/all_to_all | solution.py:189
  515.2 36.7 %all-to-all-start.10 = ((f32[16,2,2,1024]{3,1,2,0:T(2,128)}), f32[16,2,2,1024]{3,1,2,0:T(2,128)S(1)}, u32[]{:S(2)}, u32[]{:S(2)}) async-start(f32[16,2,2,1024]{3,1,2,0:T(2,128)} %copy.128), calls=%async_computation.11 | async-start | bytes 524288 | tf_op jit(solution)/shard_map/all_to_all | solution.py:201
  551.9 30.8 %all-to-all-start.7 = ((f32[16,2,64,128]{3,1,2,0:T(2,128)}), f32[16,2,64,128]{3,1,2,0:T(2,128)S(1)}, u32[]{:S(2)}, u32[]{:S(2)}) async-start(f32[16,2,64,128]{3,1,2,0:T(2,128)} %copy.117), calls=%async_computation.7 | async-start | bytes 2097152 | tf_op jit(solution)/shard_map/all_to_all | solution.py:194
Sparse Core Ops, SparseCore 0:
  252.6 212.2 reduce-scatter.1
where the time goes:
time: 594 us; the launch traced here: 592 us
  waiting for transfers between devices  322 us (54%)
  starting transfers between devices  100 us (17%)
  matrix products  60.2 us (10%)
  blocking collectives  39.6 us (7%)
  local copies, waits for them, and re-layouts  38.2 us (6%)
  between operations  14.4 us (2%)
  other arithmetic  12.6 us (2%)
    reduce_scatter x1, waiting for transfers between devices, local(): lax.psum_scatter(jnp.einsum('jyw,jaw->jya', token_rows, block_down_weight...  177 us
    all_gather x1, blocking collectives, local(): lax.all_gather(backward_rank_part.reshape(tokens_here, rank_overall), 'se...  39.6 us
    dot_general x8, matrix products, one_block(): jnp.dot(probabilities.T, grad_block, preferred_element_type=jnp.float32)  30.3 us
    all_to_all x1, waiting for transfers between devices, local(): lax.all_to_all(slot_down.reshape(group_count, capacity, rank_overall, por...  26 us
    all_to_all x1, waiting for transfers between devices, local(): lax.all_to_all(key_grid, 'seq', split_axis=1, concat_axis=0, tiled=True)  25.2 us
    all_to_all x1, starting transfers between devices, local(): lax.all_to_all(slot_up.reshape(group_count, capacity, rank_portion, value...  25 us
    all_to_all x1, waiting for transfers between devices, local(): lax.all_to_all(grad_grid, 'seq', split_axis=1, concat_axis=0, tiled=True)  22.2 us
    all_to_all x1, waiting for transfers between devices, local(): lax.all_to_all(head_grads, 'seq', split_axis=0, concat_axis=1, tiled=True)  20.3 us
  transfers between devices with their start and end apart: 12, of which 9 were waited for; matrix products, arithmetic and copies ran while one was open for 17% of the time, Pallas kernels for 0%

commit v1 on v0

--- a/solution.py
+++ b/solution.py
@@ -177,8 +177,16 @@
         adapter_scale
         * jnp.einsum("vaw,vpw->vap", value_row_blocks, near_up, preferred_element_type=jnp.float32)
     ).astype(jnp.bfloat16)
-    all_low = lax.all_gather(
-        backward_rank_part.reshape(tokens_here, rank_overall), "seq", axis=0, tiled=True
+    all_low = jnp.concatenate(
+        lax.all_to_all(
+            jnp.stack(
+                [backward_rank_part.reshape(tokens_here, rank_overall)] * lax.axis_size("seq")
+            ),
+            "seq",
+            0,
+            0,
+        ),
+        axis=0,
     )
     back_down = jnp.einsum(
         "jcy,jct->jyt",

time: 594 us -> 574 us (0.966)
  blocking collectives: 39.6 us -> 0 us
  waiting for transfers between devices: 322 us -> 340 us
  local copies, waits for them, and re-layouts: 38.2 us -> 52.6 us
  matrix products: 60.2 us -> 50.9 us
    all_gather x1 -> x0, blocking collectives: 39.6 us -> none  [local(): lax.all_gather(backward_rank_part.reshape(tokens_here, rank_overall), 'se...]
    while x0 -> x32, local copies, waits for them, and re-layouts: none -> 13.3 us
    dot_general x8, matrix products: 30.3 us -> 19.9 us  [one_block(): jnp.dot(probabilities.T, grad_block, preferred_element_type=jnp.float32)]
    all_to_all x1, waiting for transfers between devices: 0.01 us -> 9.41 us  [local(): lax.all_to_all(up_weight_terms, 'seq', split_axis=1, concat_axis=0, tiled...]
    all_to_all x0 -> x1, waiting for transfers between devices: none -> 9.32 us  [local(): lax.all_to_all(jnp.stack([backward_rank_part.reshape(tokens_here, rank_ov...]
    all_to_all x1, waiting for transfers between devices: 19.1 us -> 28.1 us  [local(): lax.all_to_all(query_grid, 'seq', split_axis=1, concat_axis=0, tiled=True)]
    all_to_all x1, starting transfers between devices: 25 us -> 16.1 us  [local(): lax.all_to_all(slot_up.reshape(group_count, capacity, rank_portion, value...]
    unnamed x18 -> x20, local copies, waits for them, and re-layouts: 14.3 us -> 14.3 us
  transfers between devices with their start and end apart: 12 -> 13, of which waited for: 9 -> 11; matrix products, arithmetic and copies ran while one was open for 17% -> 16% of each run, Pallas kernels for 0% -> 0%
where the time goes in v1:
time: 574 us; the launch traced here: 572 us
  waiting for transfers between devices  340 us (59%)
  starting transfers between devices  95.5 us (17%)
  local copies, waits for them, and re-layouts  52.6 us (9%)
  matrix products  50.9 us (9%)
  between operations  14.4 us (3%)
  other arithmetic  12.6 us (2%)
    reduce_scatter x1, waiting for transfers between devices, local(): lax.psum_scatter(jnp.einsum('jyw,jaw->jya', token_rows, block_down_weight...  176 us
    all_to_all x1, waiting for transfers between devices, local(): lax.all_to_all(query_grid, 'seq', split_axis=1, concat_axis=0, tiled=True)  28.1 us
    all_to_all x1, waiting for transfers between devices, local(): lax.all_to_all(slot_down.reshape(group_count, capacity, rank_overall, por...  26 us
    all_to_all x1, waiting for transfers between devices, local(): lax.all_to_all(key_grid, 'seq', split_axis=1, concat_axis=0, tiled=True)  22.3 us
    dot_general x8, matrix products, one_block(): jnp.dot(query_block, key_block.T, preferred_element_type=jnp.float32)  20.7 us
    all_to_all x1, waiting for transfers between devices, local(): lax.all_to_all(head_grads, 'seq', split_axis=0, concat_axis=1, tiled=True)  20.3 us
    dot_general x8, matrix products, one_block(): jnp.dot(probabilities.T, grad_block, preferred_element_type=jnp.float32)  19.9 us
    all_to_all x1, waiting for transfers between devices, local(): lax.all_to_all(grad_grid, 'seq', split_axis=1, concat_axis=0, tiled=True)  19.1 us
  transfers between devices with their start and end apart: 13, of which 11 were waited for; matrix products, arithmetic and copies ran while one was open for 16% of the time, Pallas kernels for 0%

profile of v1, /device:TPU:1, one launch (start us, length us, event | category | flops | bytes accessed | tf_op | source)
XLA Modules:
  0.0 571.7 jit_solution(17796660449488075796)
XLA Ops:
  11.0 11.8 %all-to-all-start.4 = ((bf16[16,2,2,1024]{3,2,1,0:T(2,128)(2,1)}), bf16[16,2,2,1024]{3,2,1,0:T(2,128)(2,1)S(1)}, u32[]{:S(2)}, u32[]{:S(2)}) async-start(bf16[16,2,2,1024]{3,2,1,0:T(2,128)(2,1)} %copy.107), calls=%async_computation.4 | async-start | bytes 262144 | tf_op jit(solution)/shard_map/all_to_all | solution.py:104
  25.0 7.0 %all-to-all-done.4 = bf16[16,2,2,1024]{3,2,1,0:T(2,128)(2,1)S(1)} async-done(((bf16[16,2,2,1024]{3,2,1,0:T(2,128)(2,1)}), bf16[16,2,2,1024]{3,2,1,0:T(2,128)(2,1)S(1)}, u32[]{:S(2)}, u32[]{:S(2)}) %all-to-all-start.4) | async-done | bytes 131104 | tf_op jit(solution)/shard_map/all_to_all | solution.py:104
  32.0 3.5 all-to-all-start.9
  38.4 13.9 %all-to-all-done.9 = bf16[16,2,64,128]{3,2,1,0:T(8,128)(2,1)S(1)} async-done(((bf16[16,2,64,128]{3,2,1,0:T(8,128)(2,1)}), bf16[16,2,64,128]{3,2,1,0:T(8,128)(2,1)S(1)}, u32[]{:S(2)}, u32[]{:S(2)}) %all-to-all-start.9) | async-done | bytes 524320 | tf_op jit(solution)/shard_map/all_to_all | solution.py:103
  52.3 9.7 %all-to-all-start = ((bf16[128,32,1,128]{3,0,2,1:T(8,128)(2,1)}), bf16[128,32,1,128]{3,0,2,1:T(8,128)(2,1)S(1)}, u32[]{:S(2)}, u32[]{:S(2)}) async-start(bf16[128,32,1,128]{3,0,2,1:T(8,128)(2,1)} %copy.99), calls=%async_computation | async-start | bytes 2097152 | tf_op jit(solution)/shard_map/all_to_all | solution.py:152
  62.1 28.1 %all-to-all-done = bf16[128,32,1,128]{3,0,2,1:T(8,128)(2,1)S(1)} async-done(((bf16[128,32,1,128]{3,0,2,1:T(8,128)(2,1)}), bf16[128,32,1,128]{3,0,2,1:T(8,128)(2,1)S(1)}, u32[]{:S(2)}, u32[]{:S(2)}) %all-to-all-start) | async-done | bytes 1048608 | tf_op jit(solution)/shard_map/all_to_all | solution.py:152
  91.6 5.5 all-to-all-start.1
  100.0 22.3 %all-to-all-done.1 = bf16[128,32,1,128]{3,0,2,1:T(8,128)(2,1)S(1)} async-done(((bf16[128,32,1,128]{3,0,2,1:T(8,128)(2,1)}), bf16[128,32,1,128]{3,0,2,1:T(8,128)(2,1)S(1)}, u32[]{:S(2)}, u32[]{:S(2)}) %all-to-all-start.1) | async-done | bytes 1048608 | tf_op jit(solution)/shard_map/all_to_all | solution.py:153
  122.2 8.1 %all-to-all-start.2 = ((bf16[128,32,1,128]{3,0,2,1:T(8,128)(2,1)}), bf16[128,32,1,128]{3,0,2,1:T(8,128)(2,1)}, u32[]{:S(2)}, u32[]{:S(2)}) async-start(bf16[128,32,1,128]{3,0,2,1:T(8,128)(2,1)} %copy.102), calls=%async_computation.2 | async-start | bytes 2097152 | tf_op jit(solution)/shard_map/all_to_all | solution.py:154
  135.8 19.1 %all-to-all-done.2 = bf16[128,32,1,128]{3,0,2,1:T(8,128)(2,1)} async-done(((bf16[128,32,1,128]{3,0,2,1:T(8,128)(2,1)}), bf16[128,32,1,128]{3,0,2,1:T(8,128)(2,1)}, u32[]{:S(2)}, u32[]{:S(2)}) %all-to-all-start.2) | async-done | bytes 1048608 | tf_op jit(solution)/shard_map/all_to_all | solution.py:154
  154.9 8.6 %all-to-all-start.7 = ((bf16[128,32,128]{2,0,1:T(8,128)(2,1)}), bf16[128,32,128]{2,0,1:T(8,128)(2,1)S(1)}, u32[]{:S(2)}, u32[]{:S(2)}) async-start(bf16[128,32,128]{2,0,1:T(8,128)(2,1)} %copy.111), calls=%async_computation.7 | async-start | bytes 2097152 | tf_op jit(solution)/shard_map/all_to_all | solution.py:131
  163.5 1.9 broadcast.204
  165.4 72.3 %while.19 = (s32[]{:T(128)}, f32[6144,128]{1,0:T(8,128)}, s32[8]{0:T(128)S(1)}, s32[6144]{0:T(1024)S(1)}, s32[4096]{0:T(1024)S(1)}, /*index=5*/bf16[4096,128]{1,...) while((s32[]{:T(128)}, f32[6144,128]{1,0:T(8,128)}, ...), condition=%wide.region_9.10_spmd, body=%wide.region_6.9_spmd.sunk | while | flops 685836288 | bytes 44509508 | solution.py:43
  166.8 2.6 fusion.60
  170.3 2.5 fusion.62
  172.8 1.7 copy-done.2
  175.9 2.6 fusion.60
  179.3 2.5 fusion.62
  181.8 1.7 copy-done.2
  184.9 2.6 fusion.60
  188.3 2.5 fusion.62
  190.8 1.7 copy-done.2
  193.9 2.6 fusion.60
  197.4 2.5 fusion.62
  199.9 1.7 copy-done.2
  203.0 2.6 fusion.60
  206.4 2.5 fusion.62
  212.0 2.6 fusion.60
  215.5 2.5 fusion.62
  221.1 2.6 fusion.60
  224.5 2.5 fusion.62
  230.1 2.6 fusion.60
  233.6 2.5 fusion.62
  237.7 1.7 fusion.9
  242.5 9.2 %all-to-all-start.3 = ((bf16[32,2,8192]{2,1,0:T(2,128)(2,1)}), bf16[32,2,8192]{2,1,0:T(2,128)(2,1)S(1)}, u32[]{:S(2)}, u32[]{:S(2)}) async-start(bf16[32,2,8192]{2,1,0:T(2,128)(2,1)} %reshape.256), calls=%async_computation.3 | async-start | bytes 2097152 | tf_op jit(solution)/shard_map/all_to_all | solution.py:166
  252.0 1.9 convolution_bitcast_fusion
  256.0 20.3 %all-to-all-done.3 = bf16[32,2,8192]{2,1,0:T(2,128)(2,1)S(1)} async-done(((bf16[32,2,8192]{2,1,0:T(2,128)(2,1)}), bf16[32,2,8192]{2,1,0:T(2,128)(2,1)S(1)}, u32[]{:S(2)}, u32[]{:S(2)}) %all-to-all-start.3) | async-done | bytes 1048608 | tf_op jit(solution)/shard_map/all_to_all | solution.py:166
  277.3 8.4 %all-to-all-start.5 = ((bf16[32,2,1024]{2,1,0:T(2,128)(2,1)}), bf16[32,2,1024]{2,1,0:T(2,128)(2,1)S(1)}, u32[]{:S(2)}, u32[]{:S(2)}) async-start(bf16[32,2,1024]{2,1,0:T(2,128)(2,1)} %copy.109), calls=%async_computation.5 | async-start | bytes 262144 | tf_op jit(solution)/shard_map/all_to_all | solution.py:146
  285.7 4.3 reshape.257
  292.7 176.4 %reduce-scatter.2.cloned.1.call-done = f32[128,64]{0,1:T(8,128)} async-done(((f32[4096,64]{0,1:T(8,128)}), f32[128,64]{0,1:T(8,128)}) %reduce-scatter.2.cloned.1.call-update) | async-done | bytes 32784 | tf_op jit(solution)/shard_map/reduce_scatter | solution.py:135
  471.1 6.6 %all-to-all-start.10 = ((f32[1,64,1024]{2,0,1:T(1,128)}), f32[1,64,1024]{2,0,1:T(1,128)S(1)}, u32[]{:S(2)}, u32[]{:S(2)}) async-start(f32[1,64,1024]{2,0,1:T(1,128)} %copy.123), calls=%async_computation.11 | async-start | bytes 524288 | tf_op jit(solution)/shard_map/all_to_all | solution.py:197
  477.9 9.4 %all-to-all-done.10 = f32[1,64,1024]{2,0,1:T(1,128)S(1)} async-done(((f32[1,64,1024]{2,0,1:T(1,128)}), f32[1,64,1024]{2,0,1:T(1,128)S(1)}, u32[]{:S(2)}, u32[]{:S(2)}) %all-to-all-start.10) | async-done | bytes 262176 | tf_op jit(solution)/shard_map/all_to_all | solution.py:197
  488.3 4.4 all-to-all-start.6
  494.7 9.3 %all-to-all-done.6 = bf16[32,128,64]{1,2,0:T(8,128)(2,1)S(1)} async-done(((bf16[32,128,64]{1,2,0:T(8,128)(2,1)}), bf16[32,128,64]{1,2,0:T(8,128)(2,1)S(1)}, u32[]{:S(2)}, u32[]{:S(2)}) %all-to-all-start.6) | async-done | bytes 524320 | tf_op jit(solution)/shard_map/all_to_all | solution.py:181
  504.0 16.1 %all-to-all-start.11 = ((f32[16,2,2,1024]{3,1,2,0:T(2,128)}), f32[16,2,2,1024]{3,1,2,0:T(2,128)S(1)}, u32[]{:S(2)}, u32[]{:S(2)}) async-start(f32[16,2,2,1024]{3,1,2,0:T(2,128)} %copy.125), calls=%async_computation.12 | async-start | bytes 524288 | tf_op jit(solution)/shard_map/all_to_all | solution.py:209
  523.4 8.4 %all-to-all-done.11 = f32[16,2,2,1024]{3,1,2,0:T(2,128)S(1)} async-done(((f32[16,2,2,1024]{3,1,2,0:T(2,128)}), f32[16,2,2,1024]{3,1,2,0:T(2,128)S(1)}, u32[]{:S(2)}, u32[]{:S(2)}) %all-to-all-start.11) | async-done | bytes 262176 | tf_op jit(solution)/shard_map/all_to_all | solution.py:209
  531.8 3.6 all-to-all-start.8
  536.6 26.0 %all-to-all-done.8 = f32[16,2,64,128]{3,1,2,0:T(2,128)S(1)} async-done(((f32[16,2,64,128]{3,1,2,0:T(2,128)}), f32[16,2,64,128]{3,1,2,0:T(2,128)S(1)}, u32[]{:S(2)}, u32[]{:S(2)}) %all-to-all-start.8) | async-done | bytes 1048608 | tf_op jit(solution)/shard_map/all_to_all | solution.py:202
  (151 shorter events, 59.4 us)
Async XLA Ops:
  7.2 54.8 %copy-start = (bf16[128,1024]{1,0:T(8,128)(2,1)S(1)}, bf16[128,1024]{1,0:T(8,128)(2,1)}, u32[]{:S(2)}) copy-start(bf16[128,1024]{1,0:T(8,128)(2,1)} %param.13) | copy-start | bytes 786436
  11.0 21.0 %all-to-all-start.4 = ((bf16[16,2,2,1024]{3,2,1,0:T(2,128)(2,1)}), bf16[16,2,2,1024]{3,2,1,0:T(2,128)(2,1)S(1)}, u32[]{:S(2)}, u32[]{:S(2)}) async-start(bf16[16,2,2,1024]{3,2,1,0:T(2,128)(2,1)} %copy.107), calls=%async_computation.4 | async-start | bytes 262144 | tf_op jit(solution)/shard_map/all_to_all | solution.py:104
  32.0 20.3 %all-to-all-start.9 = ((bf16[16,2,64,128]{3,2,1,0:T(8,128)(2,1)}), bf16[16,2,64,128]{3,2,1,0:T(8,128)(2,1)S(1)}, u32[]{:S(2)}, u32[]{:S(2)}) async-start(bf16[16,2,64,128]{3,2,1,0:T(8,128)(2,1)} %copy.119), calls=%async_computation.9 | async-start | bytes 1048576 | tf_op jit(solution)/shard_map/all_to_all | solution.py:103
  52.3 37.9 %all-to-all-start = ((bf16[128,32,1,128]{3,0,2,1:T(8,128)(2,1)}), bf16[128,32,1,128]{3,0,2,1:T(8,128)(2,1)S(1)}, u32[]{:S(2)}, u32[]{:S(2)}) async-start(bf16[128,32,1,128]{3,0,2,1:T(8,128)(2,1)} %copy.99), calls=%async_computation | async-start | bytes 2097152 | tf_op jit(solution)/shard_map/all_to_all | solution.py:152
  90.2 1.4 copy-start.4
  91.6 30.7 %all-to-all-start.1 = ((bf16[128,32,1,128]{3,0,2,1:T(8,128)(2,1)}), bf16[128,32,1,128]{3,0,2,1:T(8,128)(2,1)S(1)}, u32[]{:S(2)}, u32[]{:S(2)}) async-start(bf16[128,32,1,128]{3,0,2,1:T(8,128)(2,1)} %bitcast.10), calls=%async_computation.1 | async-start | bytes 2097152 | tf_op jit(solution)/shard_map/all_to_all | solution.py:153
  122.2 32.7 %all-to-all-start.2 = ((bf16[128,32,1,128]{3,0,2,1:T(8,128)(2,1)}), bf16[128,32,1,128]{3,0,2,1:T(8,128)(2,1)}, u32[]{:S(2)}, u32[]{:S(2)}) async-start(bf16[128,32,1,128]{3,0,2,1:T(8,128)(2,1)} %copy.102), calls=%async_computation.2 | async-start | bytes 2097152 | tf_op jit(solution)/shard_map/all_to_all | solution.py:154
  134.5 30.9 %copy-start.5 = (s32[32]{0:T(128)}, s32[32]{0:T(128)S(1)}, u32[]{:S(2)}) copy-start(s32[32]{0:T(128)S(1)} %select_reduce_fusion.1) | copy-start | bytes 388
  154.9 87.6 %all-to-all-start.7 = ((bf16[128,32,128]{2,0,1:T(8,128)(2,1)}), bf16[128,32,128]{2,0,1:T(8,128)(2,1)S(1)}, u32[]{:S(2)}, u32[]{:S(2)}) async-start(bf16[128,32,128]{2,0,1:T(8,128)(2,1)} %copy.111), calls=%async_computation.7 | async-start | bytes 2097152 | tf_op jit(solution)/shard_map/all_to_all | solution.py:131
  166.8 3.4 copy-start.1
  172.7 1.7 copy-start.2
  175.9 3.4 copy-start.1
  181.8 1.7 copy-start.2
  184.9 3.4 copy-start.1
  190.8 1.7 copy-start.2
  193.9 3.4 copy-start.1
  199.9 1.7 copy-start.2
  203.0 3.4 copy-start.1
  208.9 1.7 copy-start.2
  212.0 3.4 copy-start.1
  218.0 1.7 copy-start.2
  221.1 3.4 copy-start.1
  227.0 1.7 copy-start.2
  230.1 3.4 copy-start.1
  236.0 1.7 copy-start.2
  242.5 12.4 %copy-start.6 = (s32[32]{0:T(128)S(1)}, s32[32]{0:T(128)}, u32[]{:S(2)}) copy-start(s32[32]{0:T(128)} %copy-done.5) | copy-start | bytes 388
  242.5 33.7 %all-to-all-start.3 = ((bf16[32,2,8192]{2,1,0:T(2,128)(2,1)}), bf16[32,2,8192]{2,1,0:T(2,128)(2,1)S(1)}, u32[]{:S(2)}, u32[]{:S(2)}) async-start(bf16[32,2,8192]{2,1,0:T(2,128)(2,1)} %reshape.256), calls=%async_computation.3 | async-start | bytes 2097152 | tf_op jit(solution)/shard_map/all_to_all | solution.py:166
  251.8 217.4 %reduce-scatter.2.cloned.1.call-start = ((), (), s32[]{:S(2)}) async-start(), calls=%async_computation.13 | async-start | bytes 1081344 | tf_op jit(solution)/shard_map/reduce_scatter | solution.py:135
  276.2 1.0 copy-start.3
  277.3 193.8 %all-to-all-start.5 = ((bf16[32,2,1024]{2,1,0:T(2,128)(2,1)}), bf16[32,2,1024]{2,1,0:T(2,128)(2,1)S(1)}, u32[]{:S(2)}, u32[]{:S(2)}) async-start(bf16[32,2,1024]{2,1,0:T(2,128)(2,1)} %copy.109), calls=%async_computation.5 | async-start | bytes 262144 | tf_op jit(solution)/shard_map/all_to_all | solution.py:146
  291.2 202.3 %copy-start.7 = (s32[32]{0:T(128)S(1)}, s32[32]{0:T(128)}, u32[]{:S(2)}) copy-start(s32[32]{0:T(128)} %copy-done.5) | copy-start | bytes 388
  471.1 16.2 %all-to-all-start.10 = ((f32[1,64,1024]{2,0,1:T(1,128)}), f32[1,64,1024]{2,0,1:T(1,128)S(1)}, u32[]{:S(2)}, u32[]{:S(2)}) async-start(f32[1,64,1024]{2,0,1:T(1,128)} %copy.123), calls=%async_computation.11 | async-start | bytes 524288 | tf_op jit(solution)/shard_map/all_to_all | solution.py:197
  488.3 15.8 %all-to-all-start.6 = ((bf16[32,128,64]{1,2,0:T(8,128)(2,1)}), bf16[32,128,64]{1,2,0:T(8,128)(2,1)S(1)}, u32[]{:S(2)}, u32[]{:S(2)}) async-start(bf16[32,128,64]{1,2,0:T(8,128)(2,1)} %stack.3), calls=%async_computation.6 | async-start | bytes 1048576 | tf_op jit(solution)/shard_map/all_to_all | solution.py:181
  504.0 27.8 %all-to-all-start.11 = ((f32[16,2,2,1024]{3,1,2,0:T(2,128)}), f32[16,2,2,1024]{3,1,2,0:T(2,128)S(1)}, u32[]{:S(2)}, u32[]{:S(2)}) async-start(f32[16,2,2,1024]{3,1,2,0:T(2,128)} %copy.125), calls=%async_computation.12 | async-start | bytes 524288 | tf_op jit(solution)/shard_map/all_to_all | solution.py:209
  531.8 30.8 %all-to-all-start.8 = ((f32[16,2,64,128]{3,1,2,0:T(2,128)}), f32[16,2,64,128]{3,1,2,0:T(2,128)S(1)}, u32[]{:S(2)}, u32[]{:S(2)}) async-start(f32[16,2,64,128]{3,1,2,0:T(2,128)} %copy.114), calls=%async_computation.8 | async-start | bytes 2097152 | tf_op jit(solution)/shard_map/all_to_all | solution.py:202
Sparse Core Ops, SparseCore 0:
  257.0 212.1 reduce-scatter.1
